TPU v7x, 32 devices: a whole 2x2x4 slice. The times are simulated.
32 devices in a mesh: dp: 4 (over y, x), ctx: 8 (over z, core).
Axes of the slice: x: 2, y: 2, z: 4, core: 2. Of those that a mesh axis runs over, the one named last changes fastest.
Arguments:
- tokens: bfloat16 [4, 1024, 2048], P('dp', 'ctx'), may hold values from -6 to 6
- positions: int32 [4, 1024], P('dp', 'ctx'), may hold values from 0 to 1023, as said below
- norm_gain: float32 [2048], replicated, may hold values from 0.5 to 1.5
- norm_bias: float32 [2048], replicated, may hold values from -1.8 to 1.8
- qkv_weight: bfloat16 [2048, 6144], P('ctx'), may hold values from -0.125 to 0.125
- qkv_bias: float32 [6144], replicated, may hold values from -1.8 to 1.8
- dense_weight: bfloat16 [2048, 2048], P('ctx'), may hold values from -2 to 2
- dense_bias: float32 [2048], replicated, may hold values from -1.8 to 1.8
- up_weight: bfloat16 [2048, 8192], P('ctx'), may hold values from -0.125 to 0.125
- up_bias: float32 [8192], replicated, may hold values from -1.8 to 1.8
- down_weight: bfloat16 [8192, 2048], P('ctx'), may hold values from -0.0625 to 0.0625
- down_bias: float32 [2048], replicated, may hold values from -1.8 to 1.8
- clip_limit: int32 [32], replicated, may hold values from 3 to 11
- cotangent: bfloat16 [4, 1024, 2048], P('dp', 'ctx'), may hold values from -6 to 6
Outputs:
- layer_out: bfloat16 [4, 1024, 2048], P('dp', 'ctx')
- tokens_grad: float32 [4, 1024, 2048], P('dp', 'ctx')
- norm_gain_grad: float32 [2048], replicated
- norm_bias_grad: float32 [2048], replicated
- qkv_weight_grad: float32 [2048, 6144], P('ctx')
- qkv_bias_grad: float32 [6144], replicated
- dense_weight_grad: float32 [2048, 2048], P('ctx')
- dense_bias_grad: float32 [2048], replicated
- up_weight_grad: float32 [2048, 8192], P('ctx')
- up_bias_grad: float32 [8192], replicated
- down_weight_grad: float32 [8192, 2048], P('ctx')
- down_bias_grad: float32 [2048], replicated
- head_maxima: float32 [32], replicated
- clipped_weight: float32 [2048, 4096], P('ctx')
- clipped_bias: float32 [4096], replicated
Inputs may be any that keep to these rules, and one draw needn't show every extreme that they name: `positions`: within each sequence the ids rise by one from 0 at its first token and return to 0 at the first token of each packed document; the first sequence holds a single document.
All inputs are finite; a program needn't handle non-finite values.
Results may differ from a plain program's by a relative error of at most 0.017.
Values may be sent and summed in bfloat16 or wider, within the bound.
No kernel may reach another device: no remote copies, remote signals or barrier semaphores. Data moves between devices by JAX's collectives and lax.ppermute only.
A program may use at most 512 MiB of HBM per device.

v0:
```python
from functools import partial
import jax
import jax.numpy as jnp
from jax import lax
from jax.sharding import PartitionSpec as P

ROT = 32
EPSILON = 1e-05
MASKED = -1e30
ROPE_BASE = 10000.0
BF16 = jnp.bfloat16
F32 = jnp.float32


def rotary_tables(positions):
    half_rot = ROT // 2
    frequency = ROPE_BASE ** (-(jnp.arange(half_rot, dtype=F32) * 2.0 / ROT))
    angles = positions.astype(F32)[..., None] * frequency
    cosine = jnp.cos(angles)
    sine = jnp.sin(angles)
    return (
        jnp.concatenate([cosine, cosine], -1)[..., None, :],
        jnp.concatenate([sine, sine], -1)[..., None, :],
    )


def rotate(values, cosine, sine):
    half_rot = ROT // 2
    turned = values[..., :ROT]
    swapped = jnp.concatenate([-turned[..., half_rot:], turned[..., :half_rot]], -1)
    return jnp.concatenate([turned * cosine + swapped * sine, values[..., ROT:]], -1)


def rotate_back(gradient, cosine, sine):
    half_rot = ROT // 2
    turned = gradient[..., :ROT]
    scaled = turned * sine
    swapped = jnp.concatenate([scaled[..., half_rot:], -scaled[..., :half_rot]], -1)
    return jnp.concatenate([turned * cosine + swapped, gradient[..., ROT:]], -1)


def dot(left, right, contract):
    return lax.dot_general(
        left, right, ((contract[:1], contract[1:]), ((), ())), preferred_element_type=F32
    )


def per_device(
    tokens,
    positions,
    norm_gain,
    norm_bias,
    qkv_weight,
    qkv_bias,
    dense_weight,
    dense_bias,
    up_weight,
    up_bias,
    down_weight,
    down_bias,
    clip_limit,
    cotangent,
):
    seqs, stretch, width = tokens.shape
    heads = clip_limit.shape[0]
    head_dim = width // heads
    rows = seqs * stretch
    parts = lax.axis_size("ctx")
    part = lax.axis_index("ctx")
    own_heads = heads // parts
    own = own_heads * head_dim
    own_rows = qkv_weight.shape[0]
    own_ff = down_weight.shape[0]
    length = stretch * parts
    all_rows = seqs * length
    scale = head_dim ** (-0.5)
    pieces = jnp.concatenate(
        [
            qkv_weight.reshape(own_rows, 3, parts, own)
            .transpose(2, 0, 1, 3)
            .reshape(parts, own_rows, 3 * own),
            up_weight.reshape(own_rows, parts, own_ff).transpose(1, 0, 2),
        ],
        axis=2,
    )
    in_weight = lax.all_to_all(pieces, "ctx", split_axis=0, concat_axis=0, tiled=True).reshape(
        width, 3 * own + own_ff
    )
    grad_rows = lax.all_gather(cotangent, "ctx", axis=1, tiled=True).reshape(all_rows, width)
    inputs = tokens.reshape(rows, width).astype(F32)
    centre = inputs - jnp.mean(inputs, axis=-1, keepdims=True)
    inv_std = lax.rsqrt(jnp.mean(centre * centre, axis=-1, keepdims=True) + EPSILON)
    normed = centre * inv_std
    hidden_local = (normed * norm_gain + norm_bias).astype(BF16)
    hidden = lax.all_gather(
        hidden_local.reshape(seqs, stretch, width), "ctx", axis=1, tiled=True
    ).reshape(all_rows, width)
    all_positions = lax.all_gather(positions, "ctx", axis=1, tiled=True)
    qkv_own_bias = lax.dynamic_slice_in_dim(
        qkv_bias.reshape(3, parts, own), part, 1, axis=1
    ).reshape(3 * own)
    up_own_bias = lax.dynamic_slice_in_dim(up_bias, part * own_ff, own_ff)
    projected = dot(hidden, in_weight, (1, 0))
    joined = projected[:, : 3 * own] + qkv_own_bias
    upward = projected[:, 3 * own :] + up_own_bias
    cosine, sine = rotary_tables(all_positions)
    shaped = joined.reshape(seqs, length, 3, own_heads, head_dim)
    queries = rotate(shaped[:, :, 0], cosine, sine).astype(BF16)
    keys = rotate(shaped[:, :, 1], cosine, sine).astype(BF16)
    values = shaped[:, :, 2].astype(BF16)
    place = jnp.arange(length, dtype=jnp.int32)
    allowed = place[:, None] >= place[None, :]
    scores = jnp.einsum("sqhd,skhd->shqk", queries, keys, preferred_element_type=F32) * scale
    scores = jnp.where(allowed, scores, MASKED)
    row_max = jnp.max(scores, axis=-1, keepdims=True)
    expo = jnp.exp(scores - row_max)
    row_sum = jnp.sum(expo, axis=-1, keepdims=True)
    probs = expo / row_sum
    probs_low = probs.astype(BF16)
    mixed = jnp.einsum("shqk,skhd->sqhd", probs_low, values, preferred_element_type=F32)
    attended = mixed.reshape(all_rows, own).astype(BF16)
    own_maxima = jnp.max(row_max, axis=(0, 2, 3))
    slots = lax.dynamic_update_slice_in_dim(
        jnp.full((heads,), MASKED, F32), own_maxima, part * own_heads, axis=0
    )
    head_maxima = lax.pmax(slots, ("dp", "ctx"))
    activated = jax.nn.gelu(upward, approximate=True).astype(BF16)
    branch = dot(attended, dense_weight, (1, 0)) + dot(activated, down_weight, (1, 0))
    branch_sum = lax.psum_scatter(
        branch.astype(BF16).reshape(seqs, length, width), "ctx", scatter_dimension=1, tiled=True
    ).reshape(rows, width)
    layer_out = (inputs + branch_sum.astype(F32) + dense_bias + down_bias).astype(BF16)
    mixed_grad = dot(grad_rows, dense_weight, (1, 1)).astype(BF16)
    act_grad = dot(grad_rows, down_weight, (1, 1))
    dense_grad = dot(attended, grad_rows, (0, 0))
    down_grad = dot(activated, grad_rows, (0, 0))
    out_bias_grad = jnp.sum(cotangent.reshape(rows, width).astype(F32), axis=0)
    unused_value, gelu_back = jax.vjp(partial(jax.nn.gelu, approximate=True), upward)
    up_low = gelu_back(act_grad)[0].astype(BF16)
    mixed_low = mixed_grad.reshape(seqs, length, own_heads, head_dim)
    value_grad = jnp.einsum("shqk,sqhd->skhd", probs_low, mixed_low, preferred_element_type=F32)
    prob_grad = jnp.einsum("sqhd,skhd->shqk", mixed_low, values, preferred_element_type=F32)
    delta = jnp.sum(probs * prob_grad, axis=-1, keepdims=True)
    score_grad = (probs * (prob_grad - delta)).astype(BF16)
    query_grad = jnp.einsum("shqk,skhd->sqhd", score_grad, keys, preferred_element_type=F32) * scale
    key_grad = (
        jnp.einsum("shqk,sqhd->skhd", score_grad, queries, preferred_element_type=F32) * scale
    )
    joined_low = (
        jnp.stack(
            [
                rotate_back(query_grad, cosine, sine),
                rotate_back(key_grad, cosine, sine),
                value_grad,
            ],
            axis=2,
        )
        .reshape(all_rows, 3 * own)
        .astype(BF16)
    )
    both = jnp.concatenate([joined_low, up_low], axis=1)
    hidden_part = dot(both, in_weight, (1, 1))
    hidden_grad = (
        lax.psum_scatter(
            hidden_part.astype(BF16).reshape(seqs, length, width),
            "ctx",
            scatter_dimension=1,
            tiled=True,
        )
        .reshape(rows, width)
        .astype(F32)
    )
    in_grad = dot(hidden, both, (0, 0)).astype(BF16)
    in_quarter = lax.psum_scatter(
        in_grad.reshape(parts, own_rows, 3 * own + own_ff), "dp", scatter_dimension=1, tiled=True
    )
    in_quarter = lax.all_to_all(in_quarter, "ctx", split_axis=0, concat_axis=0, tiled=True)
    in_rows = lax.all_gather(in_quarter.transpose(1, 0, 2), "dp", axis=0, tiled=True)
    qkv_grad = (
        in_rows[:, :, : 3 * own]
        .reshape(own_rows, parts, 3, own)
        .transpose(0, 2, 1, 3)
        .reshape(own_rows, 3 * width)
        .astype(F32)
    )
    up_grad = in_rows[:, :, 3 * own :].reshape(own_rows, parts * own_ff).astype(F32)
    out_grad = lax.psum(jnp.concatenate([dense_grad, down_grad], axis=0).astype(BF16), "dp")
    gain_part = jnp.sum(hidden_grad * normed, axis=0)
    shift_part = jnp.sum(hidden_grad, axis=0)
    scaled = hidden_grad * norm_gain
    tokens_grad = cotangent.reshape(rows, width).astype(F32) + inv_std * (
        scaled
        - jnp.mean(scaled, axis=-1, keepdims=True)
        - normed * jnp.mean(scaled * normed, axis=-1, keepdims=True)
    )
    qkv_bias_part = lax.dynamic_update_slice(
        jnp.zeros((3, parts, own), F32),
        jnp.sum(joined_low.astype(F32), axis=0).reshape(3, 1, own),
        (0, part, 0),
    ).reshape(3 * width)
    up_bias_part = lax.dynamic_update_slice(
        jnp.zeros((parts * own_ff,), F32), jnp.sum(up_low.astype(F32), axis=0), (part * own_ff,)
    )
    gain_grad, shift_grad, qkv_bias_grad, out_bias_grad, up_bias_grad = lax.psum(
        (gain_part, shift_part, qkv_bias_part, out_bias_grad, up_bias_part), ("dp", "ctx")
    )
    limits = clip_limit.astype(F32)
    factor = limits / jnp.maximum(head_maxima, limits)
    column_scale = jnp.tile(jnp.repeat(jnp.sqrt(factor), head_dim), 2)
    clipped_weight = qkv_weight[:, : 2 * width].astype(F32) * column_scale
    clipped_bias = qkv_bias[: 2 * width] * column_scale
    return (
        layer_out.reshape(seqs, stretch, width),
        tokens_grad.reshape(seqs, stretch, width),
        gain_grad,
        shift_grad,
        qkv_grad,
        qkv_bias_grad,
        out_grad[:own].astype(F32),
        out_bias_grad,
        up_grad,
        up_bias_grad,
        out_grad[own:].astype(F32),
        out_bias_grad,
        head_maxima,
        clipped_weight,
        clipped_bias,
    )


def solution(mesh):
    rows = P("dp", "ctx", None)
    weight = P("ctx", None)
    in_specs = (rows, P("dp", "ctx"), P(), P()) + (weight, P()) * 4 + (P(), rows)
    out_specs = (rows, rows, P(), P()) + (weight, P()) * 4 + (P(), weight, P())
    return jax.shard_map(
        per_device, mesh=mesh, in_specs=in_specs, out_specs=out_specs, check_vma=False
    )
```

profile of v0, /device:TPU:0, one launch (start us, length us, event | category | flops | bytes accessed | tf_op | source)
XLA Modules:
  0.0 971.7 jit_solution(4422547686251745322)
XLA Ops:
  7.9 4.6 copy.74
  16.4 6.4 copy.76
  22.9 6.7 pad_maximum_fusion
  29.6 6.5 all-to-all-start
  38.6 174.2 %all_gather.13 = s32[1,1024]{1,0:T(1,128)S(1)} all-gather(s32[1,128]{1,0:T(1,128)S(1)} %copy-done.37), channel_id=1, replica_groups=mesh['dp'=4,'ctx'=8] {'ctx'}, dimensions={1}, use_global_device_ids=true | all-gather | bytes 4608 | tf_op jit(solution)/shard_map/all_gather | solution.py:98
  214.9 4.6 fusion.47
  219.5 29.4 %all-to-all-done = bf16[8,256,1792]{1,2,0:T(8,128)(2,1)} async-done(((bf16[8,256,1792]{1,2,0:T(8,128)(2,1)}), bf16[8,256,1792]{1,2,0:T(8,128)(2,1)}, u32[]{:S(2)}, u32[]{:S(2)}) %all-to-all-start) | async-done | bytes 7340064 | tf_op jit(solution)/shard_map/all_to_all | solution.py:86
  248.9 9.9 %copy.77 = bf16[8,256,1792]{2,1,0:T(8,128)(2,1)} copy(bf16[8,256,1792]{1,2,0:T(8,128)(2,1)} %all-to-all-done) | data formatting | bytes 14680064 | tf_op jit(solution)/shard_map/all_to_all | solution.py:86
  258.9 11.6 %fusion.22 = f32[1024,1792]{1,0:T(8,128)S(1)} fusion(bf16[2048,1792]{1,0:T(8,128)(2,1)} %bitcast.151, bf16[1,1024,2048]{2,1,0:T(8,128)(2,1)} %all-gather.4.cloned.1.call-done), kind=kOutput, calls=%fused_computation.37 | convolution fusion | flops 7516192768 | bytes 18874368 | tf_op jit(solution)/shard_map/dot_general | solution.py:43
  281.1 10.4 %fusion.95 = (f32[4,1024]{1,0:T(4,128)S(1)}, f32[4,1024,1024]{1,2,0:T(8,128)}) fusion(pred[1024,1024]{0,1:T(8,128)(4,1)S(1)} %iota_compare_fusion, bf16[1024,4,32]{0,2,1:T(8,128)(2,1)S(1)} %get-tuple-element.118, bf16[1024,4,32]{0,2,1:T(8,128)(2,1)S(1)} %get-tuple-element.104, bf16[1024,4,32]{0,2,1:T(8,128)(2,1)S(1)} %get-tuple-element.117, ...), kind=kOutput, calls=%fused_computation.150 | convolution fusion | flops 555746304 | bytes 18890752 | tf_op jit(solution)/shard_map/sub | solution.py:116
  291.6 9.6 fusion.37
  301.2 15.9 %multiply_reduce_fusion = (f32[4,1024]{1,0:T(4,128)S(1)}, f32[4,1024,1024]{1,2,0:T(8,128)}) fusion(f32[4,1024,1024]{1,2,0:T(8,128)} %get-tuple-element.112, f32[4,1024]{1,0:T(4,128)S(1)} %get-tuple-element.111, bf16[1024,4,64]{0,2,1:T(8,128)(2,1)} %bitcast.164, f32[1,1024,3,4,64]{1,4,3,2,0:T(8,128)} %bitcast.148), kind=kOutput, calls=%fused_computation.2 | convolution fusion | flops 549449728 | bytes 34635776 | tf_op jit(solution)/shard_map/sqhd,skhd->shqk/dot_general | solution.py:142
  317.1 8.0 multiply_convert_fusion
  332.5 12.3 %convert_reduce_fusion = (f32[1024]{0:T(1024)}, bf16[1024,1024]{1,0:T(8,128)(2,1)S(1)}) fusion(f32[1024]{0:T(1024)S(1)} %copy-done.35, f32[1024,1792]{1,0:T(8,128)} %copy-done.5, bf16[1024,2048]{1,0:T(8,128)(2,1)} %param.24, bf16[1,1024,2048]{2,1,0:T(8,128)(2,1)} %all-gather.6.cloned.1.call-done), kind=kOutput, calls=%fused_computation.40 | convolution fusion | flops 4319083520 | bytes 14688256 | tf_op jit(solution)/shard_map/dot_general | solution.py:43
  344.8 8.5 convolution_convert_fusion
  353.3 7.0 copy.84
  360.4 12.0 %convert_bitcast_fusion.1 = bf16[1,1024,2048]{2,1,0:T(8,128)(2,1)} fusion(bf16[2048,1792]{1,0:T(8,128)(2,1)} %bitcast.152, bf16[1024,1024]{1,0:T(8,128)(2,1)} %copy-done.42, bf16[1024,768]{1,0:T(8,128)(2,1)S(1)} %copy-done.4), kind=kOutput, calls=%fused_computation.41 | convolution fusion | flops 7525629952 | bytes 15204352 | tf_op jit(solution)/shard_map/dot_general | solution.py:43
  373.4 9.1 fusion.44
  382.5 8.5 fusion.92
  398.2 8.8 fusion.28
  409.9 38.0 %reduce-scatter.8.cloned.1.call-done = bf16[8,64,1792]{2,0,1:T(8,128)(2,1)} async-done(((bf16[8,256,1792]{2,0,1:T(8,128)(2,1)}), bf16[8,64,1792]{2,0,1:T(8,128)(2,1)}) %reduce-scatter.8.cloned.1.call-update) | async-done | bytes 1835024 | tf_op jit(solution)/shard_map/reduce_scatter | solution.py:174
  456.7 78.3 %reduce-scatter.6.cloned.1.call-done = bf16[1,128,2048]{2,1,0:T(8,128)(2,1)} async-done(((bf16[1,1024,2048]{2,1,0:T(8,128)(2,1)}), bf16[1,128,2048]{2,1,0:T(8,128)(2,1)}) %reduce-scatter.6.cloned.1.call-update) | async-done | bytes 524304 | tf_op jit(solution)/shard_map/reduce_scatter | solution.py:164
  537.1 53.5 %reduce-scatter.4.cloned.1.call-done = bf16[1,128,2048]{2,1,0:T(8,128)(2,1)} async-done(((bf16[1,1024,2048]{2,1,0:T(8,128)(2,1)}), bf16[1,128,2048]{2,1,0:T(8,128)(2,1)}) %reduce-scatter.4.cloned.1.call-update) | async-done | bytes 524304 | tf_op jit(solution)/shard_map/reduce_scatter | solution.py:129
  597.0 5.4 fusion.1
  602.5 38.0 %pmax.7 = f32[32]{0:T(128)S(1)} all-reduce(f32[32]{0:T(128)S(1)} %dynamic_update_slice.11), channel_id=1, replica_groups=mesh['dp'=4,'ctx'=8] {'dp','ctx'}, use_global_device_ids=true, to_apply=%region_22.23 | all-reduce | flops 32 | bytes 256 | tf_op jit(solution)/shard_map/pmax | solution.py:126
  645.5 69.2 %all-reduce.4.cloned.1.call-done = bf16[1280,2048]{1,0:T(8,128)(2,1)} async-done(((bf16[1280,2048]{1,0:T(8,128)(2,1)}), bf16[1280,2048]{1,0:T(8,128)(2,1)}) %all-reduce.4.cloned.1.call-update) | async-done | bytes 5242896 | tf_op jit(solution)/shard_map/psum | solution.py:187
  717.5 6.7 slice_convert_fusion
  724.1 120.5 %all-reduce.6.cloned.1.call-done = (f32[2048]{0:T(1024)}, f32[2048]{0:T(1024)}, f32[6144]{0:T(1024)}, f32[2048]{0:T(1024)}, f32[8192]{0:T(1024)}) async-done(((f32[2048]{0:T(1024)}, f32[2048]{0:T(1024)}, f32[6144]{0:T(1024)}, f32[2048]{0:T(1024)}, f32[8192]{0:T(1024)}), (f32[2048]{0:T(1024)}, f32[2048]{0:T(1024)}, f32[6144]{0:T(1024)}, f32[2048]{0:T(1024)}, f32[8192]{0:T(1024)})) %all-reduce.6.cloned.1.call-update) | async-done | bytes 81936 | tf_op jit(solution)/shard_map/psum | solution.py:204
  844.6 82.7 %all-gather.8.cloned.1.call-done = bf16[256,8,1792]{2,1,0:T(8,128)(2,1)} async-done(((bf16[64,8,1792]{2,1,0:T(8,128)(2,1)}), bf16[256,8,1792]{2,1,0:T(8,128)(2,1)}) %all-gather.8.cloned.1.call-update) | async-done | bytes 7340048 | tf_op jit(solution)/shard_map/all_gather | solution.py:178
  931.1 5.0 copy.94
  939.3 11.0 %copy.96 = f32[32,8,8,1024]{3,1,2,0:T(8,128)} copy(f32[32,8,8,1024]{3,2,1,0:T(8,128)S(1)} %bitcast.139) | data formatting | bytes 16777216
  954.4 6.6 copy.89
  (181 shorter events, 77.4 us)
Async XLA Ops:
  7.2 207.7 %copy-start = (bf16[256,2048]{1,0:T(8,128)(2,1)S(1)}, bf16[256,2048]{1,0:T(8,128)(2,1)}, u32[]{:S(2)}) copy-start(bf16[256,2048]{1,0:T(8,128)(2,1)} %param.20) | copy-start | bytes 3145732
  7.2 207.7 %all-gather.6.cloned.1.call-start = ((), (), s32[]{:S(2)}) async-start(), calls=%async_computation.7 | async-start | bytes 4718592 | tf_op jit(solution)/shard_map/all_gather | solution.py:89
  29.6 183.3 %copy-start.21 = (f32[6144]{0:T(1024)S(1)}, f32[6144]{0:T(1024)}, u32[]{:S(2)}) copy-start(f32[6144]{0:T(1024)} %param.19) | copy-start | bytes 73732
  29.6 219.4 %all-to-all-start = ((bf16[8,256,1792]{1,2,0:T(8,128)(2,1)}), bf16[8,256,1792]{1,2,0:T(8,128)(2,1)}, u32[]{:S(2)}, u32[]{:S(2)}) async-start(bf16[8,256,1792]{1,2,0:T(8,128)(2,1)} %pad_maximum_fusion), calls=%async_computation | async-start | bytes 14680064 | tf_op jit(solution)/shard_map/all_to_all | solution.py:86
  36.1 222.8 %all-gather.4.cloned.1.call-start = ((), (), s32[]{:S(2)}) async-start(), calls=%async_computation.5 | async-start | bytes 4718592 | tf_op jit(solution)/shard_map/all_gather | solution.py:95
  38.6 409.4 %reduce-scatter.8.cloned.1.call-start = ((), (), s32[]{:S(2)}) async-start(), calls=%async_computation.9 | async-start | bytes 9175040 | tf_op jit(solution)/shard_map/reduce_scatter | solution.py:174
  214.9 76.7 %copy-start.6 = (pred[1024,1024]{0,1:T(8,128)(4,1)}, pred[1024,1024]{0,1:T(8,128)(4,1)S(1)}, u32[]{:S(2)}) copy-start(pred[1024,1024]{0,1:T(8,128)(4,1)S(1)} %iota_compare_fusion) | copy-start | bytes 3145732
  280.8 92.2 %copy-start.7 = (bf16[1024,4,32]{0,2,1:T(8,128)(2,1)}, bf16[1024,4,32]{0,2,1:T(8,128)(2,1)S(1)}, u32[]{:S(2)}) copy-start(bf16[1024,4,32]{0,2,1:T(8,128)(2,1)S(1)} %get-tuple-element.117) | copy-start | bytes 786436
  301.2 15.9 %slice-start = ((s8[16777216]{0:T(1024)(128)(4,1)}), s8[4194304]{0:T(1024)(128)(4,1)S(1)}, s32[]{:S(2)}) async-start(s8[16777216]{0:T(1024)(128)(4,1)} %bitcast.142), calls=%async_computation.13 | async-start | bytes 8388608
  301.2 15.9 %slice-start.1 = ((s8[16777216]{0:T(1024)(128)(4,1)}), s8[4194304]{0:T(1024)(128)(4,1)S(1)}, s32[]{:S(2)}) async-start(s8[16777216]{0:T(1024)(128)(4,1)} %bitcast.142), calls=%async_computation.14 | async-start | bytes 8388608
  301.2 15.9 %slice-start.2 = ((s8[16777216]{0:T(1024)(128)(4,1)}), s8[4194304]{0:T(1024)(128)(4,1)S(1)}, s32[]{:S(2)}) async-start(s8[16777216]{0:T(1024)(128)(4,1)} %bitcast.142), calls=%async_computation.15 | async-start | bytes 8388608
  301.2 15.9 %slice-start.3 = ((s8[16777216]{0:T(1024)(128)(4,1)}), s8[4194304]{0:T(1024)(128)(4,1)S(1)}, s32[]{:S(2)}) async-start(s8[16777216]{0:T(1024)(128)(4,1)} %bitcast.142), calls=%async_computation.16 | async-start | bytes 8388608
  332.5 12.3 %copy-start.4 = (bf16[1024,768]{1,0:T(8,128)(2,1)S(1)}, bf16[1024,768]{1,0:T(8,128)(2,1)}, u32[]{:S(2)}) copy-start(bf16[1024,768]{1,0:T(8,128)(2,1)} %copy.83) | copy-start | bytes 4718596
  332.5 12.3 %copy-start.39 = (bf16[1,1024,2048]{2,1,0:T(8,128)(2,1)S(1)}, bf16[1,1024,2048]{2,1,0:T(8,128)(2,1)}, u32[]{:S(2)}) copy-start(bf16[1,1024,2048]{2,1,0:T(8,128)(2,1)} %all-gather.4.cloned.1.call-done) | copy-start | bytes 12582916
  360.3 174.7 %reduce-scatter.6.cloned.1.call-start = ((), (), s32[]{:S(2)}) async-start(), calls=%async_computation.8 | async-start | bytes 4718592 | tf_op jit(solution)/shard_map/reduce_scatter | solution.py:164
  372.4 218.2 %reduce-scatter.4.cloned.1.call-start = ((), (), s32[]{:S(2)}) async-start(), calls=%async_computation.6 | async-start | bytes 4718592 | tf_op jit(solution)/shard_map/reduce_scatter | solution.py:129
  394.4 320.3 %all-reduce.4.cloned.1.call-start = ((), (), s32[]{:S(2)}) async-start(), calls=%async_computation.11 | async-start | bytes 10485760 | tf_op jit(solution)/shard_map/psum | solution.py:187
  409.9 46.6 %copy-start.36 = (f32[1024]{0:T(1024)S(1)}, f32[1024]{0:T(1024)}, u32[]{:S(2)}) copy-start(f32[1024]{0:T(1024)} %get-tuple-element.115) | copy-start | bytes 12292
  409.9 125.1 %copy-start.2 = (bf16[1,128,2048]{2,1,0:T(8,128)(2,1)S(1)}, bf16[1,128,2048]{2,1,0:T(8,128)(2,1)}, u32[]{:S(2)}) copy-start(bf16[1,128,2048]{2,1,0:T(8,128)(2,1)} %param.14) | copy-start | bytes 1572868
  409.9 125.1 %copy-start.20 = (f32[2048]{0:T(1024)S(1)}, f32[2048]{0:T(1024)}, u32[]{:S(2)}) copy-start(f32[2048]{0:T(1024)} %param.16) | copy-start | bytes 24580
  409.9 125.1 %copy-start.27 = (f32[128]{0:T(128)S(1)}, f32[128]{0:T(128)}, u32[]{:S(2)}) copy-start(f32[128]{0:T(128)} %copy-done.26) | copy-start | bytes 1540
  409.9 125.1 %copy-start.34 = (f32[128]{0:T(128)S(1)}, f32[128]{0:T(128)}, u32[]{:S(2)}) copy-start(f32[128]{0:T(128)} %copy-done.33) | copy-start | bytes 1540
  409.9 180.8 %copy-start.29 = (f32[2048]{0:T(1024)S(1)}, f32[2048]{0:T(1024)}, u32[]{:S(2)}) copy-start(f32[2048]{0:T(1024)} %param.25) | copy-start | bytes 24580
  409.9 180.7 %copy-start.30 = (f32[2048]{0:T(1024)S(1)}, f32[2048]{0:T(1024)}, u32[]{:S(2)}) copy-start(f32[2048]{0:T(1024)} %param.21) | copy-start | bytes 24580
  451.0 143.6 %all-to-all-start.1 = ((bf16[8,64,1792]{2,1,0:T(8,128)(2,1)}), bf16[8,64,1792]{2,1,0:T(8,128)(2,1)S(1)}, u32[]{:S(2)}, u32[]{:S(2)}) async-start(bf16[8,64,1792]{2,1,0:T(8,128)(2,1)} %copy.85), calls=%async_computation.4 | async-start | bytes 3670016 | tf_op jit(solution)/shard_map/all_to_all | solution.py:177
  455.6 389.0 %all-reduce.6.cloned.1.call-start = ((), (), s32[]{:S(2)}) async-start(), calls=%async_computation.12 | async-start | bytes 163840 | tf_op jit(solution)/shard_map/psum | solution.py:204
  456.7 137.9 %copy-start.18 = (f32[8192]{0:T(1024)}, f32[8192]{0:T(1024)S(1)}, u32[]{:S(2)}) copy-start(f32[8192]{0:T(1024)S(1)} %dynamic_update_slice.10) | copy-start | bytes 98308
  594.6 332.7 %all-gather.8.cloned.1.call-start = ((), (), s32[]{:S(2)}) async-start(), calls=%async_computation.10 | async-start | bytes 9175040 | tf_op jit(solution)/shard_map/all_gather | solution.py:178
  597.0 43.6 %copy-start.40 = (s32[32]{0:T(128)S(1)}, s32[32]{0:T(128)}, u32[]{:S(2)}) copy-start(s32[32]{0:T(128)} %param.26) | copy-start | bytes 388
  597.0 43.7 %copy-start.22 = (f32[6144]{0:T(1024)S(1)}, f32[6144]{0:T(1024)}, u32[]{:S(2)}) copy-start(f32[6144]{0:T(1024)} %param.19) | copy-start | bytes 73732
  640.5 76.9 %copy-start.41 = (f32[32]{0:T(128)}, f32[32]{0:T(128)S(1)}, u32[]{:S(2)}) copy-start(f32[32]{0:T(128)S(1)} %pmax.7) | copy-start | bytes 388
  939.3 11.0 %copy-start.3 = (bf16[256,8,768]{0,2,1:T(8,128)(2,1)S(1)}, bf16[256,8,768]{0,2,1:T(8,128)(2,1)}, u32[]{:S(2)}) copy-start(bf16[256,8,768]{0,2,1:T(8,128)(2,1)} %copy.94) | copy-start | bytes 9437188
  (25 other events, 141.7 us)
Sparse Core Ops, SparseCore 0:
  9.6 67.6 all-gather.5
  79.5 135.0 all-gather.3
  360.5 87.4 reduce-scatter.7
  450.7 84.2 reduce-scatter.5
  537.7 52.9 reduce-scatter.3
  594.4 120.2 all-reduce.3
  722.2 122.3 all-reduce.5
  847.1 80.2 all-gather.7
where the time goes:
time: 976 us; the launch traced here: 972 us
  waiting for transfers between devices  473 us (48%)
  blocking collectives  212 us (22%)
  matrix products  128 us (13%)
  local copies, waits for them, and re-layouts  84.9 us (9%)
  other arithmetic  47 us (5%)
  between operations  15 us (2%)
  starting transfers between devices  12 us (1%)
    all_gather x1, blocking collectives, per_device(): all_positions = lax.all_gather(positions, 'ctx', axis=1, tiled=True)  174 us
    psum x1, waiting for transfers between devices, per_device(): lax.psum((gain_part, shift_part, qkv_bias_part, out_bias_grad, up_bias_pa...  121 us
    all_gather x1, waiting for transfers between devices, per_device(): lax.all_gather(in_quarter.transpose(1, 0, 2), 'dp', axis=0, tiled=True)  82.7 us
    reduce_scatter x1, waiting for transfers between devices, per_device(): lax.psum_scatter(hidden_part.astype(BF16).reshape(seqs, length, width), '...  78.3 us
    dot_general x9, matrix products, dot(): lax.dot_general(left, right, ((contract[:1], contract[1:]), ((), ())), pr...  73.4 us
    psum x1, waiting for transfers between devices, per_device(): lax.psum(jnp.concatenate([dense_grad, down_grad], axis=0).astype(BF16), '...  69.2 us
    reduce_scatter x1, waiting for transfers between devices, per_device(): lax.psum_scatter(branch.astype(BF16).reshape(seqs, length, width), 'ctx',...  53.5 us
    unnamed x108, local copies, waits for them, and re-layouts  42.9 us
  transfers between devices with their start and end apart: 10, of which 7 were waited for; matrix products, arithmetic and copies ran while one was open for 12% of the time, Pallas kernels for 0%

commit v1 on v0

--- a/solution.py
+++ b/solution.py
@@ -184,7 +184,8 @@
         .astype(F32)
     )
     up_grad = in_rows[:, :, 3 * own :].reshape(own_rows, parts * own_ff).astype(F32)
-    out_grad = lax.psum(jnp.concatenate([dense_grad, down_grad], axis=0).astype(BF16), "dp")
+    body = jnp.concatenate([dense_grad, down_grad], axis=0).astype(BF16)
+    out_grad = lax.all_gather(body, "dp").sum(axis=0)
     gain_part = jnp.sum(hidden_grad * normed, axis=0)
     shift_part = jnp.sum(hidden_grad, axis=0)
     scaled = hidden_grad * norm_gain

time: 976 us -> 1040 us (1.066)
  waiting for transfers between devices: 473 us -> 517 us
  other arithmetic: 47 us -> 63.1 us
    all_gather x0 -> x1, waiting for transfers between devices: none -> 160 us  [per_device(): out_grad = lax.all_gather(body, 'dp').sum(axis=0)]
    psum x1 -> x0, waiting for transfers between devices: 69.2 us -> none  [per_device(): lax.psum(jnp.concatenate([dense_grad, down_grad], axis=0).astype(BF16), '...]
    psum x1, waiting for transfers between devices: 121 us -> 58.9 us  [per_device(): lax.psum((gain_part, shift_part, qkv_bias_part, out_bias_grad, up_bias_pa...]
    reduce_scatter x1, waiting for transfers between devices: 38 us -> 53.3 us  [per_device(): lax.psum_scatter(in_grad.reshape(parts, own_rows, 3 * own + own_ff), 'dp'...]
    reduce_sum x0 -> x1, other arithmetic: none -> 14.8 us  [per_device(): out_grad = lax.all_gather(body, 'dp').sum(axis=0)]
    unnamed x108 -> x120, local copies, waits for them, and re-layouts: 42.9 us -> 44.7 us
  transfers between devices with their start and end apart: 10 -> 10, of which waited for: 7 -> 7; matrix products, arithmetic and copies ran while one was open for 12% -> 14% of each run, Pallas kernels for 0% -> 0%
where the time goes in v1:
time: 1040 us; the launch traced here: 1030 us
  waiting for transfers between devices  517 us (50%)
  blocking collectives  212 us (20%)
  matrix products  126 us (12%)
  local copies, waits for them, and re-layouts  86.9 us (8%)
  other arithmetic  63.1 us (6%)
  between operations  15.3 us (1%)
  starting transfers between devices  11.6 us (1%)
    all_gather x1, blocking collectives, per_device(): all_positions = lax.all_gather(positions, 'ctx', axis=1, tiled=True)  174 us
    all_gather x1, waiting for transfers between devices, per_device(): out_grad = lax.all_gather(body, 'dp').sum(axis=0)  160 us
    all_gather x1, waiting for transfers between devices, per_device(): lax.all_gather(in_quarter.transpose(1, 0, 2), 'dp', axis=0, tiled=True)  82.7 us
    reduce_scatter x1, waiting for transfers between devices, per_device(): lax.psum_scatter(hidden_part.astype(BF16).reshape(seqs, length, width), '...  78.1 us
    dot_general x9, matrix products, dot(): lax.dot_general(left, right, ((contract[:1], contract[1:]), ((), ())), pr...  73.3 us
    psum x1, waiting for transfers between devices, per_device(): lax.psum((gain_part, shift_part, qkv_bias_part, out_bias_grad, up_bias_pa...  58.9 us
    reduce_scatter x1, waiting for transfers between devices, per_device(): lax.psum_scatter(branch.astype(BF16).reshape(seqs, length, width), 'ctx',...  53.4 us
    reduce_scatter x1, waiting for transfers between devices, per_device(): lax.psum_scatter(in_grad.reshape(parts, own_rows, 3 * own + own_ff), 'dp'...  53.3 us
  transfers between devices with their start and end apart: 10, of which 7 were waited for; matrix products, arithmetic and copies ran while one was open for 14% of the time, Pallas kernels for 0%

profile of v1, /device:TPU:0, one launch (start us, length us, event | category | flops | bytes accessed | tf_op | source)
XLA Modules:
  0.0 1031.6 jit_solution(18341694140487957121)
XLA Ops:
  7.9 4.6 copy.74
  16.4 6.4 copy.76
  22.9 6.7 pad_maximum_fusion
  29.6 6.5 all-to-all-start
  38.6 174.2 %all_gather.17 = s32[1,1024]{1,0:T(1,128)S(1)} all-gather(s32[1,128]{1,0:T(1,128)S(1)} %copy-done.43), channel_id=1, replica_groups=mesh['dp'=4,'ctx'=8] {'ctx'}, dimensions={1}, use_global_device_ids=true | all-gather | bytes 4608 | tf_op jit(solution)/shard_map/all_gather | solution.py:98
  214.9 4.6 fusion.49
  219.5 29.4 %all-to-all-done = bf16[8,256,1792]{1,2,0:T(8,128)(2,1)} async-done(((bf16[8,256,1792]{1,2,0:T(8,128)(2,1)}), bf16[8,256,1792]{1,2,0:T(8,128)(2,1)}, u32[]{:S(2)}, u32[]{:S(2)}) %all-to-all-start) | async-done | bytes 7340064 | tf_op jit(solution)/shard_map/all_to_all | solution.py:86
  248.9 9.9 copy.77
  258.9 11.7 %fusion.22 = f32[1024,1792]{1,0:T(8,128)S(1)} fusion(bf16[2048,1792]{1,0:T(8,128)(2,1)} %bitcast.157, bf16[1,1024,2048]{2,1,0:T(8,128)(2,1)} %all-gather.5.cloned.1.call-done), kind=kOutput, calls=%fused_computation.37 | convolution fusion | flops 7516192768 | bytes 18874368 | tf_op jit(solution)/shard_map/dot_general | solution.py:43
  281.1 10.1 fusion.97
  291.3 9.6 fusion.39
  300.9 15.9 %multiply_reduce_fusion = (f32[4,1024]{1,0:T(4,128)S(1)}, f32[4,1024,1024]{1,2,0:T(8,128)}) fusion(f32[4,1024,1024]{1,2,0:T(8,128)} %get-tuple-element.112, f32[4,1024]{1,0:T(4,128)S(1)} %get-tuple-element.111, bf16[1024,4,64]{0,2,1:T(8,128)(2,1)} %bitcast.170, f32[1,1024,3,4,64]{1,4,3,2,0:T(8,128)} %bitcast.154), kind=kOutput, calls=%fused_computation.2 | convolution fusion | flops 549449728 | bytes 34635776 | tf_op jit(solution)/shard_map/sqhd,skhd->shqk/dot_general | solution.py:142
  316.8 8.1 multiply_convert_fusion
  332.2 12.3 %convert_reduce_fusion = (f32[1024]{0:T(1024)}, bf16[1024,1024]{1,0:T(8,128)(2,1)S(1)}) fusion(f32[1024]{0:T(1024)S(1)} %copy-done.40, f32[1024,1792]{1,0:T(8,128)} %copy-done.5, bf16[1024,2048]{1,0:T(8,128)(2,1)} %param.24, bf16[1,1024,2048]{2,1,0:T(8,128)(2,1)} %all-gather.7.cloned.1.call-done), kind=kOutput, calls=%fused_computation.40 | convolution fusion | flops 4319083520 | bytes 14688256 | tf_op jit(solution)/shard_map/dot_general | solution.py:43
  344.5 8.7 convolution_convert_fusion
  353.2 7.0 copy.84
  360.3 12.0 %convert_bitcast_fusion.2 = bf16[1,1024,2048]{2,1,0:T(8,128)(2,1)} fusion(bf16[2048,1792]{1,0:T(8,128)(2,1)} %bitcast.158, bf16[1024,1024]{1,0:T(8,128)(2,1)} %copy-done.48, bf16[1024,768]{1,0:T(8,128)(2,1)S(1)} %copy-done.4), kind=kOutput, calls=%fused_computation.42 | convolution fusion | flops 7525629952 | bytes 15204352 | tf_op jit(solution)/shard_map/dot_general | solution.py:43
  373.3 9.1 fusion.46
  382.4 8.7 fusion.94
  394.6 53.3 %reduce-scatter.8.cloned.1.call-done = bf16[8,64,1792]{2,0,1:T(8,128)(2,1)} async-done(((bf16[8,256,1792]{2,0,1:T(8,128)(2,1)}), bf16[8,64,1792]{2,0,1:T(8,128)(2,1)}) %reduce-scatter.8.cloned.1.call-update) | async-done | bytes 1835024 | tf_op jit(solution)/shard_map/reduce_scatter | solution.py:174
  456.8 78.1 %reduce-scatter.6.cloned.1.call-done = bf16[1,128,2048]{2,1,0:T(8,128)(2,1)} async-done(((bf16[1,1024,2048]{2,1,0:T(8,128)(2,1)}), bf16[1,128,2048]{2,1,0:T(8,128)(2,1)}) %reduce-scatter.6.cloned.1.call-update) | async-done | bytes 524304 | tf_op jit(solution)/shard_map/reduce_scatter | solution.py:164
  537.0 53.4 %reduce-scatter.4.cloned.1.call-done = bf16[1,128,2048]{2,1,0:T(8,128)(2,1)} async-done(((bf16[1,1024,2048]{2,1,0:T(8,128)(2,1)}), bf16[1,128,2048]{2,1,0:T(8,128)(2,1)}) %reduce-scatter.4.cloned.1.call-update) | async-done | bytes 524304 | tf_op jit(solution)/shard_map/reduce_scatter | solution.py:129
  600.4 8.4 convert_bitcast_fusion.1
  616.5 38.1 %pmax.7 = f32[32]{0:T(128)S(1)} all-reduce(f32[32]{0:T(128)S(1)} %dynamic_update_slice.11), channel_id=1, replica_groups=mesh['dp'=4,'ctx'=8] {'dp','ctx'}, use_global_device_ids=true, to_apply=%region_22.23 | all-reduce | flops 32 | bytes 256 | tf_op jit(solution)/shard_map/pmax | solution.py:126
  659.5 58.9 %all-reduce.3.cloned.1.call-done = (f32[2048]{0:T(1024)}, f32[2048]{0:T(1024)}, f32[6144]{0:T(1024)}, f32[2048]{0:T(1024)}, f32[8192]{0:T(1024)}) async-done(((f32[2048]{0:T(1024)}, f32[2048]{0:T(1024)}, f32[6144]{0:T(1024)}, f32[2048]{0:T(1024)}, f32[8192]{0:T(1024)}), (f32[2048]{0:T(1024)}, f32[2048]{0:T(1024)}, f32[6144]{0:T(1024)}, f32[2048]{0:T(1024)}, f32[8192]{0:T(1024)})) %all-reduce.3.cloned.1.call-update) | async-done | bytes 81936 | tf_op jit(solution)/shard_map/psum | solution.py:205
  718.4 82.7 %all-gather.9.cloned.1.call-done = bf16[256,8,1792]{2,1,0:T(8,128)(2,1)} async-done(((bf16[64,8,1792]{2,1,0:T(8,128)(2,1)}), bf16[256,8,1792]{2,1,0:T(8,128)(2,1)}) %all-gather.9.cloned.1.call-update) | async-done | bytes 7340048 | tf_op jit(solution)/shard_map/all_gather | solution.py:178
  804.9 4.9 copy.94
  814.2 11.0 %copy.96 = f32[32,8,8,1024]{3,1,2,0:T(8,128)} copy(f32[32,8,8,1024]{3,2,1,0:T(8,128)S(1)} %bitcast.145) | data formatting | bytes 16777216
  829.3 6.8 copy.89
  836.2 160.0 %all-gather.11.cloned.1.call-done = bf16[4,1280,2048]{2,1,0:T(8,128)(2,1)} async-done(((bf16[1,1280,2048]{2,1,0:T(8,128)(2,1)}), bf16[4,1280,2048]{2,1,0:T(8,128)(2,1)}) %all-gather.11.cloned.1.call-update) | async-done | bytes 20971536 | tf_op jit(solution)/shard_map/all_gather | solution.py:188
  996.2 14.8 %reduce_sum.120 = bf16[1280,2048]{1,0:T(8,128)(2,1)} reduce(bf16[4,1280,2048]{2,1,0:T(8,128)(2,1)} %all-gather.11.cloned.1.call-done, bf16[]{:T(256)} %constant.54.clone.1), dimensions={0}, to_apply=%region_16.17 | reduce | flops 7864320 | bytes 26214402 | tf_op jit(solution)/shard_map/reduce_sum | solution.py:188
  1013.9 6.7 slice_convert_fusion
  (194 shorter events, 83.5 us)
Async XLA Ops:
  7.2 207.7 %copy-start = (bf16[256,2048]{1,0:T(8,128)(2,1)S(1)}, bf16[256,2048]{1,0:T(8,128)(2,1)}, u32[]{:S(2)}) copy-start(bf16[256,2048]{1,0:T(8,128)(2,1)} %param.20) | copy-start | bytes 3145732
  7.2 207.7 %all-gather.7.cloned.1.call-start = ((), (), s32[]{:S(2)}) async-start(), calls=%async_computation.7 | async-start | bytes 4718592 | tf_op jit(solution)/shard_map/all_gather | solution.py:89
  29.6 183.3 %copy-start.26 = (f32[6144]{0:T(1024)S(1)}, f32[6144]{0:T(1024)}, u32[]{:S(2)}) copy-start(f32[6144]{0:T(1024)} %param.19) | copy-start | bytes 73732
  29.6 219.4 %all-to-all-start = ((bf16[8,256,1792]{1,2,0:T(8,128)(2,1)}), bf16[8,256,1792]{1,2,0:T(8,128)(2,1)}, u32[]{:S(2)}, u32[]{:S(2)}) async-start(bf16[8,256,1792]{1,2,0:T(8,128)(2,1)} %pad_maximum_fusion), calls=%async_computation | async-start | bytes 14680064 | tf_op jit(solution)/shard_map/all_to_all | solution.py:86
  36.1 222.8 %all-gather.5.cloned.1.call-start = ((), (), s32[]{:S(2)}) async-start(), calls=%async_computation.5 | async-start | bytes 4718592 | tf_op jit(solution)/shard_map/all_gather | solution.py:95
  38.6 409.3 %reduce-scatter.8.cloned.1.call-start = ((), (), s32[]{:S(2)}) async-start(), calls=%async_computation.9 | async-start | bytes 9175040 | tf_op jit(solution)/shard_map/reduce_scatter | solution.py:174
  214.9 76.4 %copy-start.6 = (pred[1024,1024]{0,1:T(8,128)(4,1)}, pred[1024,1024]{0,1:T(8,128)(4,1)S(1)}, u32[]{:S(2)}) copy-start(pred[1024,1024]{0,1:T(8,128)(4,1)S(1)} %iota_compare_fusion) | copy-start | bytes 3145732
  280.8 91.8 %copy-start.8 = (bf16[1024,4,32]{0,2,1:T(8,128)(2,1)}, bf16[1024,4,32]{0,2,1:T(8,128)(2,1)S(1)}, u32[]{:S(2)}) copy-start(bf16[1024,4,32]{0,2,1:T(8,128)(2,1)S(1)} %get-tuple-element.117) | copy-start | bytes 786436
  300.8 15.9 %slice-start = ((s8[16777216]{0:T(1024)(128)(4,1)}), s8[4194304]{0:T(1024)(128)(4,1)S(1)}, s32[]{:S(2)}) async-start(s8[16777216]{0:T(1024)(128)(4,1)} %bitcast.148), calls=%async_computation.13 | async-start | bytes 8388608
  300.8 15.9 %slice-start.1 = ((s8[16777216]{0:T(1024)(128)(4,1)}), s8[4194304]{0:T(1024)(128)(4,1)S(1)}, s32[]{:S(2)}) async-start(s8[16777216]{0:T(1024)(128)(4,1)} %bitcast.148), calls=%async_computation.14 | async-start | bytes 8388608
  300.8 15.9 %slice-start.2 = ((s8[16777216]{0:T(1024)(128)(4,1)}), s8[4194304]{0:T(1024)(128)(4,1)S(1)}, s32[]{:S(2)}) async-start(s8[16777216]{0:T(1024)(128)(4,1)} %bitcast.148), calls=%async_computation.15 | async-start | bytes 8388608
  300.9 15.9 %slice-start.3 = ((s8[16777216]{0:T(1024)(128)(4,1)}), s8[4194304]{0:T(1024)(128)(4,1)S(1)}, s32[]{:S(2)}) async-start(s8[16777216]{0:T(1024)(128)(4,1)} %bitcast.148), calls=%async_computation.16 | async-start | bytes 8388608
  332.2 12.3 %copy-start.4 = (bf16[1024,768]{1,0:T(8,128)(2,1)S(1)}, bf16[1024,768]{1,0:T(8,128)(2,1)}, u32[]{:S(2)}) copy-start(bf16[1024,768]{1,0:T(8,128)(2,1)} %copy.83) | copy-start | bytes 4718596
  332.2 12.3 %copy-start.45 = (bf16[1,1024,2048]{2,1,0:T(8,128)(2,1)S(1)}, bf16[1,1024,2048]{2,1,0:T(8,128)(2,1)}, u32[]{:S(2)}) copy-start(bf16[1,1024,2048]{2,1,0:T(8,128)(2,1)} %all-gather.5.cloned.1.call-done) | copy-start | bytes 12582916
  360.2 174.6 %reduce-scatter.6.cloned.1.call-start = ((), (), s32[]{:S(2)}) async-start(), calls=%async_computation.8 | async-start | bytes 4718592 | tf_op jit(solution)/shard_map/reduce_scatter | solution.py:164
  372.3 218.1 %reduce-scatter.4.cloned.1.call-start = ((), (), s32[]{:S(2)}) async-start(), calls=%async_computation.6 | async-start | bytes 4718592 | tf_op jit(solution)/shard_map/reduce_scatter | solution.py:129
  394.5 62.0 %copy-start.42 = (f32[1024]{0:T(1024)S(1)}, f32[1024]{0:T(1024)}, u32[]{:S(2)}) copy-start(f32[1024]{0:T(1024)} %get-tuple-element.115) | copy-start | bytes 12292
  394.5 140.4 %copy-start.2 = (bf16[1,128,2048]{2,1,0:T(8,128)(2,1)S(1)}, bf16[1,128,2048]{2,1,0:T(8,128)(2,1)}, u32[]{:S(2)}) copy-start(bf16[1,128,2048]{2,1,0:T(8,128)(2,1)} %param.14) | copy-start | bytes 1572868
  394.5 140.4 %copy-start.25 = (f32[2048]{0:T(1024)S(1)}, f32[2048]{0:T(1024)}, u32[]{:S(2)}) copy-start(f32[2048]{0:T(1024)} %param.16) | copy-start | bytes 24580
  394.5 140.3 %copy-start.32 = (f32[128]{0:T(128)S(1)}, f32[128]{0:T(128)}, u32[]{:S(2)}) copy-start(f32[128]{0:T(128)} %copy-done.31) | copy-start | bytes 1540
  394.5 140.3 %copy-start.39 = (f32[128]{0:T(128)S(1)}, f32[128]{0:T(128)}, u32[]{:S(2)}) copy-start(f32[128]{0:T(128)} %copy-done.38) | copy-start | bytes 1540
  394.6 195.9 %copy-start.34 = (f32[2048]{0:T(1024)S(1)}, f32[2048]{0:T(1024)}, u32[]{:S(2)}) copy-start(f32[2048]{0:T(1024)} %param.25) | copy-start | bytes 24580
  394.6 195.9 %copy-start.35 = (f32[2048]{0:T(1024)S(1)}, f32[2048]{0:T(1024)}, u32[]{:S(2)}) copy-start(f32[2048]{0:T(1024)} %param.21) | copy-start | bytes 24580
  450.9 143.5 %all-to-all-start.1 = ((bf16[8,64,1792]{2,1,0:T(8,128)(2,1)}), bf16[8,64,1792]{2,1,0:T(8,128)(2,1)S(1)}, u32[]{:S(2)}, u32[]{:S(2)}) async-start(bf16[8,64,1792]{2,1,0:T(8,128)(2,1)} %copy.85), calls=%async_computation.4 | async-start | bytes 3670016 | tf_op jit(solution)/shard_map/all_to_all | solution.py:177
  455.5 262.9 %all-reduce.3.cloned.1.call-start = ((), (), s32[]{:S(2)}) async-start(), calls=%async_computation.12 | async-start | bytes 163840 | tf_op jit(solution)/shard_map/psum | solution.py:205
  456.8 137.6 %copy-start.23 = (f32[8192]{0:T(1024)}, f32[8192]{0:T(1024)S(1)}, u32[]{:S(2)}) copy-start(f32[8192]{0:T(1024)S(1)} %dynamic_update_slice.10) | copy-start | bytes 98308
  594.4 206.8 %all-gather.9.cloned.1.call-start = ((), (), s32[]{:S(2)}) async-start(), calls=%async_computation.10 | async-start | bytes 9175040 | tf_op jit(solution)/shard_map/all_gather | solution.py:178
  596.7 399.5 %all-gather.11.cloned.1.call-start = ((), (), s32[]{:S(2)}) async-start(), calls=%async_computation.11 | async-start | bytes 26214400 | tf_op jit(solution)/shard_map/all_gather | solution.py:188
  613.0 41.6 %copy-start.46 = (s32[32]{0:T(128)S(1)}, s32[32]{0:T(128)}, u32[]{:S(2)}) copy-start(s32[32]{0:T(128)} %param.26) | copy-start | bytes 388
  613.0 41.8 %copy-start.27 = (f32[6144]{0:T(1024)S(1)}, f32[6144]{0:T(1024)}, u32[]{:S(2)}) copy-start(f32[6144]{0:T(1024)} %param.19) | copy-start | bytes 73732
  654.6 150.3 %copy-start.47 = (f32[32]{0:T(128)}, f32[32]{0:T(128)S(1)}, u32[]{:S(2)}) copy-start(f32[32]{0:T(128)S(1)} %pmax.7) | copy-start | bytes 388
  814.2 11.0 %copy-start.3 = (bf16[256,8,768]{0,2,1:T(8,128)(2,1)S(1)}, bf16[256,8,768]{0,2,1:T(8,128)(2,1)}, u32[]{:S(2)}) copy-start(bf16[256,8,768]{0,2,1:T(8,128)(2,1)} %copy.94) | copy-start | bytes 9437188
  (31 other events, 158.3 us)
Sparse Core Ops, SparseCore 0:
  9.6 67.6 all-gather.6
  79.5 135.0 all-gather.4
  360.4 87.4 reduce-scatter.7
  450.6 84.2 reduce-scatter.5
  537.6 52.8 reduce-scatter.3
  597.9 120.5 all-reduce.2
  720.9 80.2 all-gather.8
  803.0 193.1 all-gather.10
